TPU v7x, 512 devices: a whole 4x4x16 slice. The times are simulated.
512 devices in a mesh: seq: 32 (over z, core), mp: 16 (over y, x).
Axes of the slice: x: 4, y: 4, z: 16, core: 2. Of those that a mesh axis runs over, the one named last changes fastest.
Arguments:
- continued_prompt_entries: bfloat16 [4096, 4096], P('seq', 'mp'), may hold values from -6 to 6
- padded_prompt_entries: bfloat16 [4096, 4096], P('seq', 'mp'), may hold values from -6 to 6
- prompt_live_extents: int32 [64], P('seq'), may hold values from 8 to 64, as said below
- preceding_entry_line: bfloat16 [4096], P('mp'), may hold values from -6 to 6
- carried_memory: float32 [64, 64, 64], P('mp'), may hold values from -24 to 24
- token_mixing_ratios: float32 [5, 4096], replicated, may hold values from 0.05 to 0.95
- acceptance_transform: bfloat16 [4096, 4096], P('seq', 'mp'), may hold values from -0.09375 to 0.09375
- lookup_transform: bfloat16 [4096, 4096], P('seq', 'mp'), may hold values from -0.09375 to 0.09375
- payload_transform: bfloat16 [4096, 4096], P('seq', 'mp'), may hold values from -0.09375 to 0.09375
- gating_transform: bfloat16 [4096, 4096], P('seq', 'mp'), may hold values from -0.09375 to 0.09375
- fading_baseline: float32 [4096], P('mp'), may hold values from -10 to -3.5
- fading_left_factor: bfloat16 [4096, 128], replicated, may hold values from -0.09375 to 0.09375
- fading_right_factor: bfloat16 [128, 4096], P(None, 'mp'), may hold values from -0.5 to 0.5
- present_reward: float32 [64, 64], P('mp'), may hold values from -3 to 3
- group_layer_scaling: float32 [4096], P('mp'), may hold values from 0.5 to 1.5
- group_layer_shift_term: float32 [4096], P('mp'), may hold values from -1.8 to 1.8
- final_transform: bfloat16 [4096, 4096], P('mp', 'seq'), may hold values from -0.09375 to 0.09375
Outputs:
- mixed: bfloat16 [32, 256, 4096], P('seq', 'mp')
- span_states: float32 [32, 64, 64, 64], P('seq', 'mp')
- request_states: float32 [64, 64, 64, 64], P('seq', 'mp')
Inputs may be any that keep to these rules, and one draw needn't show every extreme that they name: `prompt_live_extents`: some request has all 64 rows live.
All inputs are finite; a program needn't handle non-finite values.
Results may differ from a plain program's by a relative error of at most 0.0076.
Values may be sent and summed in bfloat16 or wider, within the bound.
A program may use at most 64 MiB of HBM per device.

v0:
```python
import jax
import jax.numpy as jnp
from jax import lax
from jax.sharding import PartitionSpec as P

BLK = 64
SEQ = ("z", "core")
norm_eps = 0.00064
highest = lax.Precision.HIGHEST


def seq_index():
    return lax.axis_index("z") * lax.axis_size("core") + lax.axis_index("core")


def seq_shift(x, by, length):
    pairs = [(i, i + by) for i in range(length) if i + by < length]
    return lax.ppermute(x, SEQ, pairs)


def exclusive_prefix(value, start, length):
    mine = seq_index()
    arrived = seq_shift(value, 1, length)
    total = jax.tree.map(lambda got, first: jnp.where(mine == 0, first, got), arrived, start)
    step = 1
    while step < length:
        got = seq_shift(total, step, length)
        joined = combine(got, total)
        total = jax.tree.map(lambda new, old: jnp.where(mine >= step, new, old), joined, total)
        step *= 2
    return total


def mix_rows(current, previous, weight):
    here = current.astype(jnp.float32)
    return (here + weight[None, :] * (previous.astype(jnp.float32) - here)).astype(jnp.bfloat16)


def block_sweep(
    evolving_memory,
    acceptance_entries,
    lookup_entries,
    payload_entries,
    log_fading_amount,
    diagonal_reward,
):
    inclusive = jnp.cumsum(log_fading_amount, axis=0)
    exclusive = inclusive - log_fading_amount
    recept_scaled = acceptance_entries * jnp.exp(exclusive)
    keys_scaled = lookup_entries * jnp.exp(-inclusive)
    scores = jnp.einsum("ihc,jhc->hij", recept_scaled, keys_scaled, precision=highest)
    count = acceptance_entries.shape[0]
    row_index = lax.broadcasted_iota(jnp.int32, (count, count), 0)
    col_index = lax.broadcasted_iota(jnp.int32, (count, count), 1)
    scores = jnp.where((row_index > col_index)[None], scores, 0.0)
    diagonal_contribution = jnp.sum(
        acceptance_entries * diagonal_reward[None] * lookup_entries, axis=-1, keepdims=True
    )
    answer_lines = (
        jnp.einsum("hij,jhd->ihd", scores, payload_entries, precision=highest)
        + diagonal_contribution * payload_entries
    )
    answer_lines = answer_lines + jnp.einsum(
        "ihc,hcd->ihd", recept_scaled, evolving_memory, precision=highest
    )
    total = inclusive[-1]
    carried = lookup_entries * jnp.exp(total[None] - inclusive)
    new_state = jnp.exp(total)[:, :, None] * evolving_memory + jnp.einsum(
        "jhc,jhd->hcd", carried, payload_entries, precision=highest
    )
    return (new_state, answer_lines)


def continued_recurrence(
    acceptance_entries, lookup_entries, payload_entries, log_fading_amount, diagonal_reward
):
    length, per_group_view, embedding_dimension = acceptance_entries.shape
    blocks = length // BLK

    def step(evolving_memory, entry_lines):
        return block_sweep(
            evolving_memory,
            entry_lines[0],
            entry_lines[1],
            entry_lines[2],
            entry_lines[3],
            diagonal_reward,
        )

    shaped = tuple(
        (
            a.reshape(blocks, BLK, per_group_view, embedding_dimension)
            for a in (acceptance_entries, lookup_entries, payload_entries, log_fading_amount)
        )
    )
    evolving_memory, results = lax.scan(
        step,
        jnp.zeros((per_group_view, embedding_dimension, embedding_dimension), jnp.float32),
        shaped,
    )
    return (evolving_memory, results.reshape(length, per_group_view, embedding_dimension))


def combine(earlier, later):
    return (earlier[0] + later[0], jnp.exp(later[0])[:, :, None] * earlier[1] + later[1])


def shifted_rows(current, edge_row, long_rows, requests, slot_rows):
    feature_part = current.shape[1]
    long_prev = jnp.concatenate([edge_row, current[: long_rows - 1]], axis=0)
    short_view = current[long_rows:].reshape(requests, slot_rows, feature_part)
    short_prev = jnp.concatenate(
        [jnp.zeros((requests, 1, feature_part), current.dtype), short_view[:, :-1]], axis=1
    )
    short_prev = short_prev.reshape(requests * slot_rows, feature_part)
    return jnp.concatenate([long_prev, short_prev], axis=0)


def on_device(
    continued_prompt_entries,
    padded_prompt_entries,
    prompt_live_extents,
    preceding_entry_line,
    carried_memory,
    token_mixing_ratios,
    acceptance_transform,
    lookup_transform,
    payload_transform,
    gating_transform,
    fading_baseline,
    fading_left_factor,
    fading_right_factor,
    present_reward,
    group_layer_scaling,
    group_layer_shift_term,
    final_transform,
):
    long_rows = continued_prompt_entries.shape[0]
    requests = prompt_live_extents.shape[0]
    slot_rows = padded_prompt_entries.shape[0] // requests
    per_group_view, embedding_dimension = present_reward.shape
    seq_count = lax.axis_size("z") * lax.axis_size("core")
    arrived = seq_shift(continued_prompt_entries[-1:], 1, seq_count)
    first = seq_index() == 0
    edge_row = jnp.where(first, preceding_entry_line[None, :], arrived)
    stacked = jnp.concatenate([continued_prompt_entries, padded_prompt_entries, edge_row], axis=0)
    stacked = lax.all_gather(stacked, "mp", axis=1, tiled=True)
    current = stacked[: long_rows + padded_prompt_entries.shape[0]]
    edge_full = stacked[-1:]
    previous = shifted_rows(current, edge_full, long_rows, requests, slot_rows)
    mixes = [mix_rows(current, previous, token_mixing_ratios[index]) for index in range(5)]
    total_rows = current.shape[0]
    columns = acceptance_transform.shape[1]
    blocks = jnp.stack(
        [
            acceptance_transform,
            lookup_transform,
            payload_transform,
            gating_transform,
            final_transform.T,
        ],
        axis=0,
    )
    blocks = lax.all_gather(lax.all_gather(blocks, "z"), "core")
    cores, chips, kinds, depth, width = blocks.shape
    blocks = jnp.transpose(blocks, (2, 1, 0, 3, 4)).reshape(kinds, chips * cores * depth, width)
    pieces = tuple((blocks[index] for index in range(4)))
    acceptance_entries, lookup_entries, payload_entries, gate = tuple(
        (
            jnp.dot(source, piece, preferred_element_type=jnp.float32)
            for source, piece in zip(mixes[:4], pieces)
        )
    )
    squeezed = jnp.tanh(
        jnp.dot(mixes[4], fading_left_factor, preferred_element_type=jnp.float32)
    ).astype(jnp.bfloat16)
    log_fading_amount = -jnp.exp(
        fading_baseline[None, :]
        + jnp.dot(squeezed, fading_right_factor, preferred_element_type=jnp.float32)
    )
    recept3, keys3, values3, decay3 = [
        a.reshape(total_rows, per_group_view, embedding_dimension)
        for a in (acceptance_entries, lookup_entries, payload_entries, log_fading_amount)
    ]
    local_state, long_out = continued_recurrence(
        recept3[:long_rows],
        keys3[:long_rows],
        values3[:long_rows],
        decay3[:long_rows],
        present_reward,
    )
    long_decay = decay3[:long_rows]
    group_total = jnp.sum(long_decay, axis=0)
    start = (jnp.zeros((per_group_view, embedding_dimension), jnp.float32), carried_memory)
    _, incoming = exclusive_prefix((group_total, local_state), start, seq_count)
    before_row = jnp.cumsum(long_decay, axis=0) - long_decay
    long_out = long_out + jnp.einsum(
        "ihc,hcd->ihd", recept3[:long_rows] * jnp.exp(before_row), incoming, precision=highest
    )
    span_end = jnp.exp(group_total)[:, :, None] * incoming + local_state
    live_rows = (
        lax.broadcasted_iota(jnp.int32, (requests, slot_rows), 1) < prompt_live_extents[:, None]
    )
    live_flat = live_rows.reshape(requests * slot_rows).astype(jnp.float32)[:, None, None]
    short_shape = (requests, slot_rows, per_group_view, embedding_dimension)
    short_recept = recept3[long_rows:].reshape(short_shape)
    short_keys = (keys3[long_rows:] * live_flat).reshape(short_shape)
    short_values = values3[long_rows:].reshape(short_shape)
    short_decay = (decay3[long_rows:] * live_flat).reshape(short_shape)
    zeroed_memory = jnp.zeros(
        (per_group_view, embedding_dimension, embedding_dimension), jnp.float32
    )

    def request_pass(acceptance_lines, lookup_table, payload_table, fading_table):
        return block_sweep(
            zeroed_memory,
            acceptance_lines,
            lookup_table,
            payload_table,
            fading_table,
            present_reward,
        )

    request_states, short_out = jax.vmap(request_pass)(
        short_recept, short_keys, short_values, short_decay
    )
    wkv = jnp.concatenate(
        [long_out, short_out.reshape(requests * slot_rows, per_group_view, embedding_dimension)],
        axis=0,
    )
    mean = jnp.mean(wkv, axis=-1, keepdims=True)
    centred = wkv - mean
    variance = jnp.mean(centred * centred, axis=-1, keepdims=True)
    normed = (centred * lax.rsqrt(variance + norm_eps)).reshape(
        total_rows, columns
    ) * group_layer_scaling[None, :] + group_layer_shift_term[None, :]
    row_live = jnp.concatenate(
        [jnp.ones((long_rows,), dtype=bool), live_rows.reshape(requests * slot_rows)], axis=0
    )
    hidden = jnp.where(row_live[:, None], normed * jax.nn.silu(gate), 0.0).astype(jnp.bfloat16)
    full_out = blocks[4]
    mixed_rows = lax.psum_scatter(
        lax.dot_general(
            hidden, full_out, (((1,), (1,)), ((), ())), preferred_element_type=jnp.float32
        ),
        "mp",
        scatter_dimension=0,
        tiled=True,
    )
    return (mixed_rows.astype(jnp.bfloat16)[None], span_end[None], request_states)


def solution(mesh):
    placed = (
        P("seq", "mp"),
        P("seq", "mp"),
        P("seq"),
        P("mp"),
        P("mp", None, None),
        P(),
        P("seq", "mp"),
        P("seq", "mp"),
        P("seq", "mp"),
        P("seq", "mp"),
        P("mp"),
        P(),
        P(None, "mp"),
        P("mp", None),
        P("mp"),
        P("mp"),
        P("mp", "seq"),
    )
    devices = mesh.devices
    seq_devices, mp_devices = devices.shape
    mesh = jax.sharding.Mesh(devices.reshape(seq_devices // 2, 2, mp_devices), ("z", "core", "mp"))
    placed = tuple((P(*[SEQ if name == "seq" else name for name in spec]) for spec in placed))
    return jax.shard_map(
        on_device,
        mesh=mesh,
        in_specs=placed,
        out_specs=(P(SEQ, "mp", None), P(SEQ, "mp", None, None), P(SEQ, "mp", None, None)),
        check_vma=False,
    )
```

profile of v0, /device:TPU:2, one launch (start us, length us, event | category | flops | bytes accessed | tf_op | source)
XLA Modules:
  0.0 407.3 jit_solution(4726152788664702614)
XLA Ops:
  17.9 80.3 %all-gather.8.cloned.1.call-done = bf16[80,128,256]{2,1,0:T(8,128)(2,1)} async-done(((bf16[5,128,256]{2,1,0:T(8,128)(2,1)}), bf16[80,128,256]{2,1,0:T(8,128)(2,1)}) %all-gather.8.cloned.1.call-update) | async-done | bytes 5242896 | tf_op jit(solution)/shard_map/all_gather | solution.py:164
  99.8 60.9 %all-gather.6.cloned.1.call-done = bf16[257,4096]{1,0:T(8,128)(2,1)} async-done(((bf16[257,256]{1,0:T(8,128)(2,1)}), bf16[257,4096]{1,0:T(8,128)(2,1)}) %all-gather.6.cloned.1.call-update) | async-done | bytes 2105360 | tf_op jit(solution)/shard_map/all_gather | solution.py:147
  160.7 1.9 slice-done
  164.0 3.0 fusion.40
  169.3 4.1 %collective-permute-start.2 = (f32[4,64]{1,0:T(4,128)S(1)}, f32[4,64]{1,0:T(4,128)S(1)}, u32[]{:S(2)}, u32[]{:S(2)}) collective-permute-start(f32[4,64]{1,0:T(4,128)S(1)} %get-tuple-element.130), channel_id=1, source_target_pairs={{0,16},{16,32},{32,48},{48,64},{64,80},{80,96},{96,112},{112,128},... | collective-permute-start | bytes 3080 | tf_op jit(solution)/shard_map/ppermute | solution.py:18
  174.4 6.0 %collective-permute-start.3 = (f32[4,64]{1,0:T(4,128)S(1)}, f32[4,64]{1,0:T(4,128)S(1)}, u32[]{:S(2)}, u32[]{:S(2)}) collective-permute-start(f32[4,64]{1,0:T(4,128)S(1)} %get-tuple-element.128), channel_id=1, source_target_pairs={{0,32},{16,48},{32,64},{48,80},{64,96},{80,112},{96,128},{112,144}... | collective-permute-start | bytes 3080 | tf_op jit(solution)/shard_map/ppermute | solution.py:18
  181.8 5.2 %collective-permute-start.4 = (f32[4,64]{1,0:T(4,128)S(1)}, f32[4,64]{1,0:T(4,128)S(1)}, u32[]{:S(2)}, u32[]{:S(2)}) collective-permute-start(f32[4,64]{1,0:T(4,128)S(1)} %get-tuple-element.126), channel_id=1, source_target_pairs={{0,64},{16,80},{32,96},{48,112},{64,128},{80,144},{96,160},{112,17... | collective-permute-start | bytes 3080 | tf_op jit(solution)/shard_map/ppermute | solution.py:18
  188.2 13.1 %collective-permute-start.5 = (f32[4,64]{1,0:T(4,128)S(1)}, f32[4,64]{1,0:T(4,128)S(1)}, u32[]{:S(2)}, u32[]{:S(2)}) collective-permute-start(f32[4,64]{1,0:T(4,128)S(1)} %get-tuple-element.124), channel_id=1, source_target_pairs={{0,128},{16,144},{32,160},{48,176},{64,192},{80,208},{96,224},{112... | collective-permute-start | bytes 3080 | tf_op jit(solution)/shard_map/ppermute | solution.py:18
  201.4 6.2 %fusion.92 = (bf16[1,16,2,128,256]{4,3,0,1,2:T(8,128)(2,1)}, bf16[1,16,2,128,256]{4,3,0,1,2:T(8,128)(2,1)}, bf16[1,16,2,128,256]{4,3,0,1,2:T(8,128)(2,1)S(1)}, b...) fusion(bf16[5,16,2,128,256]{4,3,0,1,2:T(8,128)(2,1)} %bitcast.142), kind=kLoop, calls=%fused_computation.139 | loop fusion | bytes 20971520 | tf_op jit(solution)/shard_map/slice | solution.py:167
  217.1 13.2 %while.13 = (s32[]{:T(128)}, f32[4,64,64]{2,1,0:T(8,128)S(1)}, f32[2,64,4,64]{1,0,3,2:T(2,128)}, f32[2,64,4,64]{1,0,3,2:T(2,128)S(1)}, f32[2,64,4,64]{3,2,1,0:T(...) while((s32[]{:T(128)}, f32[4,64,64]{2,1,0:T(8,128)S(1)}, ...), condition=%wide.region_3.4_spmd.clone, body=%wide.region_0.3_spmd.clone.sunk | while | flops 51646208 | bytes 2444424 | solution.py:96
  219.4 4.3 %dynamic_update_slice.6 = f32[2,64,4,64]{1,0,3,2:T(2,128)} dynamic-update-slice(f32[2,64,4,64]{1,0,3,2:T(2,128)} %get-tuple-element.235, f32[1,64,4,64]{1,0,3,2:T(1,128)S(1)} %copy.218, s32[]{:T(128)S(6)} %copy.227, s32[]{:T(128)} %constant.28.clone.1..sunk, s32[]{:T(128)} %constant.28.clone.1..sunk, s32[]{:T(128)} %constant.28.clone.1..sunk) | dynamic-update-slice | bytes 131076 | tf_op jit(solution)/shard_map/while/body/jit(dynamic_update_index_in_dim)/dynamic_update_slice | solution.py:96
  226.1 4.3 %dynamic_update_slice.6 = f32[2,64,4,64]{1,0,3,2:T(2,128)} dynamic-update-slice(f32[2,64,4,64]{1,0,3,2:T(2,128)} %get-tuple-element.235, f32[1,64,4,64]{1,0,3,2:T(1,128)S(1)} %copy.218, s32[]{:T(128)S(6)} %copy.227, s32[]{:T(128)} %constant.28.clone.1..sunk, s32[]{:T(128)} %constant.28.clone.1..sunk, s32[]{:T(128)} %constant.28.clone.1..sunk) | dynamic-update-slice | bytes 131076 | tf_op jit(solution)/shard_map/while/body/jit(dynamic_update_index_in_dim)/dynamic_update_slice | solution.py:96
  236.5 2.1 exponential_multiply_fusion
  238.6 5.3 %collective-permute-start.8 = (f32[4,64,64]{2,1,0:T(8,128)S(1)}, f32[4,64,64]{2,1,0:T(8,128)S(1)}, u32[]{:S(2)}, u32[]{:S(2)}) collective-permute-start(f32[4,64,64]{2,1,0:T(8,128)S(1)} %add_select_fusion.4), channel_id=1, source_target_pairs={{0,32},{16,48},{32,64},{48,80},{64,96},{80,112},{96,128},{112,144}... | collective-permute-start | bytes 196616 | tf_op jit(solution)/shard_map/ppermute | solution.py:18
  244.9 2.5 collective-permute-done.8
  247.5 6.3 %collective-permute-start.9 = (f32[4,64,64]{2,1,0:T(8,128)S(1)}, f32[4,64,64]{2,1,0:T(8,128)S(1)}, u32[]{:S(2)}, u32[]{:S(2)}) collective-permute-start(f32[4,64,64]{2,1,0:T(8,128)S(1)} %add_select_fusion.3), channel_id=1, source_target_pairs={{0,64},{16,80},{32,96},{48,112},{64,128},{80,144},{96,160},{112,17... | collective-permute-start | bytes 196616 | tf_op jit(solution)/shard_map/ppermute | solution.py:18
  254.4 3.2 collective-permute-done.9
  257.7 12.6 %collective-permute-start.10 = (f32[4,64,64]{2,1,0:T(8,128)S(1)}, f32[4,64,64]{2,1,0:T(8,128)S(1)}, u32[]{:S(2)}, u32[]{:S(2)}) collective-permute-start(f32[4,64,64]{2,1,0:T(8,128)S(1)} %add_select_fusion.2), channel_id=1, source_target_pairs={{0,128},{16,144},{32,160},{48,176},{64,192},{80,208},{96,224},{112... | collective-permute-start | bytes 196616 | tf_op jit(solution)/shard_map/ppermute | solution.py:18
  273.0 13.9 %collective-permute-start.11 = (f32[4,64,64]{2,1,0:T(8,128)S(1)}, f32[4,64,64]{2,1,0:T(8,128)}, u32[]{:S(2)}, u32[]{:S(2)}) collective-permute-start(f32[4,64,64]{2,1,0:T(8,128)S(1)} %add_select_fusion.1), channel_id=1, source_target_pairs={{0,256},{16,272},{32,288},{48,304},{64,320},{80,336},{96,352},{112... | collective-permute-start | bytes 196616 | tf_op jit(solution)/shard_map/ppermute | solution.py:18
  289.5 3.3 copy.156
  296.4 1.8 concatenate.27
  302.4 1.8 copy.154
  307.5 7.5 %fusion.68 = f32[256,4096]{1,0:T(8,128)} fusion(bf16[4096,256]{1,0:T(8,128)(2,1)} %bitcast.145, f32[256,256]{1,0:T(8,128)} %copy.154, f32[256,256]{1,0:T(8,128)} %copy.153, f32[128,256]{1,0:T(8,128)} %concatenate.27, f32[128,256]{1,0:T(8,128)} %copy.151, bf16[4096,256]{1,0:T(8,128)(2,1)} %bitcast.146, f32[4096]{0:T(1024)S(1)} %bitcast.160, ...), kind=kOutput, calls=%fused_computation.84 | convolution fusion | flops 1086062592 | bytes 13396480 | tf_op jit(solution)/shard_map/dot_general | solution.py:243
  319.0 80.1 %reduce-scatter.2.cloned.1.call-done = f32[16,4096]{1,0:T(8,128)} async-done(((f32[256,4096]{1,0:T(8,128)}), f32[16,4096]{1,0:T(8,128)}) %reduce-scatter.2.cloned.1.call-update) | async-done | bytes 262160 | tf_op jit(solution)/shard_map/reduce_scatter | solution.py:242
  (199 shorter events, 62.9 us)
Async XLA Ops:
  7.2 156.8 %copy-start = (bf16[4096,128]{1,0:T(8,128)(2,1)S(1)}, bf16[4096,128]{1,0:T(8,128)(2,1)}, u32[]{:S(2)}) copy-start(bf16[4096,128]{1,0:T(8,128)(2,1)} %param.30) | copy-start | bytes 3145732
  7.2 91.1 %all-gather.8.cloned.1.call-start = ((), (), s32[]{:S(2)}) async-start(), calls=%async_computation.3 | async-start | bytes 5570560 | tf_op jit(solution)/shard_map/all_gather | solution.py:164
  12.4 148.3 %all-gather.6.cloned.1.call-start = ((), (), s32[]{:S(2)}) async-start(), calls=%async_computation.1 | async-start | bytes 2297856 | tf_op jit(solution)/shard_map/all_gather | solution.py:147
  13.1 2.5 collective-permute-start
  17.9 183.5 %all-gather.10.cloned.1.call-start = ((), (), s32[]{:S(2)}) async-start(), calls=%async_computation.4 | async-start | bytes 15728640 | tf_op jit(solution)/shard_map/all_gather | solution.py:164
  98.3 300.9 %reduce-scatter.2.cloned.1.call-start = ((), (), s32[]{:S(2)}) async-start(), calls=%async_computation.2 | async-start | bytes 4456448 | tf_op jit(solution)/shard_map/reduce_scatter | solution.py:242
  167.2 2.1 collective-permute-start.1
  169.3 5.1 %collective-permute-start.2 = (f32[4,64]{1,0:T(4,128)S(1)}, f32[4,64]{1,0:T(4,128)S(1)}, u32[]{:S(2)}, u32[]{:S(2)}) collective-permute-start(f32[4,64]{1,0:T(4,128)S(1)} %get-tuple-element.130), channel_id=1, source_target_pairs={{0,16},{16,32},{32,48},{48,64},{64,80},{80,96},{96,112},{112,128},... | collective-permute-start | bytes 3080 | tf_op jit(solution)/shard_map/ppermute | solution.py:18
  174.4 33.2 %copy-start.7 = (f32[2,64,4,64]{3,2,1,0:T(4,128)}, f32[2,64,4,64]{3,2,1,0:T(4,128)S(1)}, u32[]{:S(2)}) copy-start(f32[2,64,4,64]{3,2,1,0:T(4,128)S(1)} %copy.141) | copy-start | bytes 393220
  174.4 7.3 %collective-permute-start.3 = (f32[4,64]{1,0:T(4,128)S(1)}, f32[4,64]{1,0:T(4,128)S(1)}, u32[]{:S(2)}, u32[]{:S(2)}) collective-permute-start(f32[4,64]{1,0:T(4,128)S(1)} %get-tuple-element.128), channel_id=1, source_target_pairs={{0,32},{16,48},{32,64},{48,80},{64,96},{80,112},{96,128},{112,144}... | collective-permute-start | bytes 3080 | tf_op jit(solution)/shard_map/ppermute | solution.py:18
  181.8 6.5 %collective-permute-start.4 = (f32[4,64]{1,0:T(4,128)S(1)}, f32[4,64]{1,0:T(4,128)S(1)}, u32[]{:S(2)}, u32[]{:S(2)}) collective-permute-start(f32[4,64]{1,0:T(4,128)S(1)} %get-tuple-element.126), channel_id=1, source_target_pairs={{0,64},{16,80},{32,96},{48,112},{64,128},{80,144},{96,160},{112,17... | collective-permute-start | bytes 3080 | tf_op jit(solution)/shard_map/ppermute | solution.py:18
  188.2 43.4 %collective-permute-start.5 = (f32[4,64]{1,0:T(4,128)S(1)}, f32[4,64]{1,0:T(4,128)S(1)}, u32[]{:S(2)}, u32[]{:S(2)}) collective-permute-start(f32[4,64]{1,0:T(4,128)S(1)} %get-tuple-element.124), channel_id=1, source_target_pairs={{0,128},{16,144},{32,160},{48,176},{64,192},{80,208},{96,224},{112... | collective-permute-start | bytes 3080 | tf_op jit(solution)/shard_map/ppermute | solution.py:18
  230.3 3.7 collective-permute-start.6
  232.7 11.8 %copy-start.19 = (f32[128,256]{1,0:T(8,128)S(1)}, f32[128,256]{1,0:T(8,128)}, u32[]{:S(2)}) copy-start(f32[128,256]{1,0:T(8,128)} %get-tuple-element.152) | copy-start | bytes 393220
  235.0 3.5 collective-permute-start.7
  238.6 8.7 %collective-permute-start.8 = (f32[4,64,64]{2,1,0:T(8,128)S(1)}, f32[4,64,64]{2,1,0:T(8,128)S(1)}, u32[]{:S(2)}, u32[]{:S(2)}) collective-permute-start(f32[4,64,64]{2,1,0:T(8,128)S(1)} %add_select_fusion.4), channel_id=1, source_target_pairs={{0,32},{16,48},{32,64},{48,80},{64,96},{80,112},{96,128},{112,144}... | collective-permute-start | bytes 196616 | tf_op jit(solution)/shard_map/ppermute | solution.py:18
  244.8 43.8 %copy-start.5 = (f32[2,64,4,64]{1,3,2,0:T(8,128)}, f32[2,64,4,64]{1,3,2,0:T(8,128)S(1)}, u32[]{:S(2)}) copy-start(f32[2,64,4,64]{1,3,2,0:T(8,128)S(1)} %copy.145) | copy-start | bytes 393220
  247.5 10.1 %collective-permute-start.9 = (f32[4,64,64]{2,1,0:T(8,128)S(1)}, f32[4,64,64]{2,1,0:T(8,128)S(1)}, u32[]{:S(2)}, u32[]{:S(2)}) collective-permute-start(f32[4,64,64]{2,1,0:T(8,128)S(1)} %add_select_fusion.3), channel_id=1, source_target_pairs={{0,64},{16,80},{32,96},{48,112},{64,128},{80,144},{96,160},{112,17... | collective-permute-start | bytes 196616 | tf_op jit(solution)/shard_map/ppermute | solution.py:18
  257.7 15.1 %collective-permute-start.10 = (f32[4,64,64]{2,1,0:T(8,128)S(1)}, f32[4,64,64]{2,1,0:T(8,128)S(1)}, u32[]{:S(2)}, u32[]{:S(2)}) collective-permute-start(f32[4,64,64]{2,1,0:T(8,128)S(1)} %add_select_fusion.2), channel_id=1, source_target_pairs={{0,128},{16,144},{32,160},{48,176},{64,192},{80,208},{96,224},{112... | collective-permute-start | bytes 196616 | tf_op jit(solution)/shard_map/ppermute | solution.py:18
  273.0 19.8 %copy-start.9 = (f32[4,64,64]{2,1,0:T(8,128)}, f32[4,64,64]{2,1,0:T(8,128)S(1)}, u32[]{:S(2)}) copy-start(f32[4,64,64]{2,1,0:T(8,128)S(1)} %add_select_fusion.1) | copy-start | bytes 196612
  273.0 26.8 %collective-permute-start.11 = (f32[4,64,64]{2,1,0:T(8,128)S(1)}, f32[4,64,64]{2,1,0:T(8,128)}, u32[]{:S(2)}, u32[]{:S(2)}) collective-permute-start(f32[4,64,64]{2,1,0:T(8,128)S(1)} %add_select_fusion.1), channel_id=1, source_target_pairs={{0,256},{16,272},{32,288},{48,304},{64,320},{80,336},{96,352},{112... | collective-permute-start | bytes 196616 | tf_op jit(solution)/shard_map/ppermute | solution.py:18
  289.5 8.7 %copy-start.1 = (bf16[1,16,2,128,256]{4,3,0,1,2:T(8,128)(2,1)S(1)}, bf16[1,16,2,128,256]{4,3,0,1,2:T(8,128)(2,1)}, u32[]{:S(2)}) copy-start(bf16[1,16,2,128,256]{4,3,0,1,2:T(8,128)(2,1)} %get-tuple-element.137) | copy-start | bytes 6291460
  299.7 7.7 %copy-start.31 = (f32[256]{0:T(256)S(1)}, f32[256]{0:T(256)}, u32[]{:S(2)}) copy-start(f32[256]{0:T(256)} %param.33) | copy-start | bytes 3076
  299.7 7.7 %copy-start.32 = (pred[256]{0:T(512)(128)(4,1)S(1)}, pred[256]{0:T(512)(128)(4,1)}, u32[]{:S(2)}) copy-start(pred[256]{0:T(512)(128)(4,1)} %concatenate.22) | copy-start | bytes 772
  (26 other events, 71.3 us)
Sparse Core Ops, SparseCore 0:
  12.5 85.6 all-gather.7
  101.8 58.8 all-gather.5
  162.8 33.1 all-gather.9
  315.1 83.9 reduce-scatter.1
where the time goes:
time: 409 us; the launch traced here: 407 us
  waiting for transfers between devices  232 us (57%)
  starting transfers between devices  72.5 us (18%)
  local copies, waits for them, and re-layouts  54.7 us (13%)
  matrix products  21.7 us (5%)
  between operations  14.5 us (4%)
  other arithmetic  11.6 us (3%)
    all_gather x2, waiting for transfers between devices, on_device(): blocks = lax.all_gather(lax.all_gather(blocks, 'z'), 'core')  80.3 us
    reduce_scatter x1, waiting for transfers between devices, on_device(): lax.psum_scatter(lax.dot_general(hidden, full_out, (((1,), (1,)), ((), ()...  80.1 us
    ppermute x12, starting transfers between devices, seq_shift(): return lax.ppermute(x, SEQ, pairs)  72.3 us
    all_gather x1, waiting for transfers between devices, on_device(): stacked = lax.all_gather(stacked, 'mp', axis=1, tiled=True)  60.9 us
    ppermute x12, waiting for transfers between devices, seq_shift(): return lax.ppermute(x, SEQ, pairs)  10.7 us
    unnamed x71, local copies, waits for them, and re-layouts  10.1 us
    dynamic_update_slice x4, local copies, waits for them, and re-layouts, continued_recurrence(): lax.scan(step, jnp.zeros((per_group_view, embedding_dimension, embedding_...  8.76 us
  transfers between devices with their start and end apart: 16, of which 10 were waited for; matrix products, arithmetic and copies ran while one was open for 14% of the time, Pallas kernels for 0%

commit v1 on v0

--- a/solution.py
+++ b/solution.py
@@ -7,6 +7,11 @@
 SEQ = ("z", "core")
 norm_eps = 0.00064
 highest = lax.Precision.HIGHEST
+
+
+def tiled_gather(x, axis, dim):
+    copies = jnp.concatenate([x] * lax.axis_size(axis), axis=dim)
+    return lax.all_to_all(copies, axis, dim, dim, tiled=True)
 
 
 def seq_index():
@@ -144,7 +149,7 @@
     first = seq_index() == 0
     edge_row = jnp.where(first, preceding_entry_line[None, :], arrived)
     stacked = jnp.concatenate([continued_prompt_entries, padded_prompt_entries, edge_row], axis=0)
-    stacked = lax.all_gather(stacked, "mp", axis=1, tiled=True)
+    stacked = tiled_gather(stacked, "mp", 1)
     current = stacked[: long_rows + padded_prompt_entries.shape[0]]
     edge_full = stacked[-1:]
     previous = shifted_rows(current, edge_full, long_rows, requests, slot_rows)

time: 409 us -> 420 us (1.027)
  waiting for transfers between devices: 232 us -> 204 us
  local copies, waits for them, and re-layouts: 54.7 us -> 80.9 us
  other arithmetic: 11.6 us -> 30.6 us
  starting transfers between devices: 72.5 us -> 67.8 us
    all_gather x1 -> x0, waiting for transfers between devices: 60.9 us -> none  [on_device(): stacked = lax.all_gather(stacked, 'mp', axis=1, tiled=True)]
    all_to_all x0 -> x1, waiting for transfers between devices: none -> 28.5 us  [tiled_gather(): return lax.all_to_all(copies, axis, dim, dim, tiled=True)]
    convert_element_type x0 -> x2, other arithmetic: none -> 12.7 us  [mix_rows(): (here + weight[None, :] * (previous.astype(jnp.float32) - here)).astype(j...]
    ppermute x12, starting transfers between devices: 72.3 us -> 60.5 us  [seq_shift(): return lax.ppermute(x, SEQ, pairs)]
    unnamed x71 -> x82, local copies, waits for them, and re-layouts: 10.1 us -> 18.4 us
    all_to_all x0 -> x1, starting transfers between devices: none -> 7.24 us  [tiled_gather(): return lax.all_to_all(copies, axis, dim, dim, tiled=True)]
    all_gather x2, waiting for transfers between devices: 80.3 us -> 85.8 us  [on_device(): blocks = lax.all_gather(lax.all_gather(blocks, 'z'), 'core')]
    ppermute x12, waiting for transfers between devices: 10.7 us -> 5.83 us  [seq_shift(): return lax.ppermute(x, SEQ, pairs)]
  transfers between devices with their start and end apart: 16 -> 16, of which waited for: 10 -> 7; matrix products, arithmetic and copies ran while one was open for 14% -> 26% of each run, Pallas kernels for 0% -> 0%
where the time goes in v1:
time: 420 us; the launch traced here: 418 us
  waiting for transfers between devices  204 us (49%)
  local copies, waits for them, and re-layouts  80.9 us (19%)
  starting transfers between devices  67.8 us (16%)
  other arithmetic  30.6 us (7%)
  matrix products  19.2 us (5%)
  between operations  14.5 us (3%)
    all_gather x2, waiting for transfers between devices, on_device(): blocks = lax.all_gather(lax.all_gather(blocks, 'z'), 'core')  85.8 us
    reduce_scatter x1, waiting for transfers between devices, on_device(): lax.psum_scatter(lax.dot_general(hidden, full_out, (((1,), (1,)), ((), ()...  84.3 us
    ppermute x12, starting transfers between devices, seq_shift(): return lax.ppermute(x, SEQ, pairs)  60.5 us
    all_to_all x1, waiting for transfers between devices, tiled_gather(): return lax.all_to_all(copies, axis, dim, dim, tiled=True)  28.5 us
    unnamed x82, local copies, waits for them, and re-layouts  18.4 us
    convert_element_type x2, other arithmetic, mix_rows(): (here + weight[None, :] * (previous.astype(jnp.float32) - here)).astype(j...  12.7 us
    slice x5, local copies, waits for them, and re-layouts, on_device(): pieces = tuple((blocks[index] for index in range(4)))  9.57 us
    dynamic_update_slice x4, local copies, waits for them, and re-layouts, continued_recurrence(): lax.scan(step, jnp.zeros((per_group_view, embedding_dimension, embedding_...  8.78 us
  transfers between devices with their start and end apart: 16, of which 7 were waited for; matrix products, arithmetic and copies ran while one was open for 26% of the time, Pallas kernels for 0%

profile of v1, /device:TPU:2, one launch (start us, length us, event | category | flops | bytes accessed | tf_op | source)
XLA Modules:
  0.0 417.7 jit_solution(12254407610293321944)
XLA Ops:
  12.4 85.8 %all-gather.5.cloned.1.call-done = bf16[80,128,256]{2,1,0:T(8,128)(2,1)} async-done(((bf16[5,128,256]{2,1,0:T(8,128)(2,1)}), bf16[80,128,256]{2,1,0:T(8,128)(2,1)}) %all-gather.5.cloned.1.call-update) | async-done | bytes 5242896 | tf_op jit(solution)/shard_map/all_gather | solution.py:169
  104.4 7.2 %all-to-all-start = ((bf16[257,16,256]{2,0,1:T(8,128)(2,1)}), bf16[257,16,256]{2,0,1:T(8,128)(2,1)S(1)}, u32[]{:S(2)}, u32[]{:S(2)}) async-start(bf16[257,16,256]{2,0,1:T(8,128)(2,1)} %copy.211), calls=%async_computation | async-start | bytes 4325376 | tf_op jit(solution)/shard_map/all_to_all | solution.py:14
  113.8 28.5 %all-to-all-done = bf16[257,16,256]{2,0,1:T(8,128)(2,1)S(1)} async-done(((bf16[257,16,256]{2,0,1:T(8,128)(2,1)}), bf16[257,16,256]{2,0,1:T(8,128)(2,1)S(1)}, u32[]{:S(2)}, u32[]{:S(2)}) %all-to-all-start) | async-done | bytes 2105376 | tf_op jit(solution)/shard_map/all_to_all | solution.py:14
  154.3 2.8 copy.257
  161.8 4.5 %fusion.22 = bf16[256,4096]{0,1:T(8,128)(2,1)} fusion(bf16[256,16,256]{0,2,1:T(8,128)(2,1)S(1)} %copy.257, bf16[128,4096]{0,1:T(8,128)(2,1)} %copy.216, bf16[127,4096]{0,1:T(8,128)(2,1)} %bitcast.167, bf16[1,4096]{0,1:T(8,128)(2,1)} %bitcast.166, f32[4096]{0:T(1024)S(1)} %bitcast.187), kind=kLoop, calls=%fused_computation.44 | loop fusion | flops 11534336 | bytes 6307840 | tf_op jit(solution)/shard_map/convert_element_type | solution.py:41
  169.8 2.6 collective-permute-start.1
  178.4 2.6 copy.217
  183.7 8.1 %fusion.20 = (bf16[256,16,256]{0,2,1:T(8,128)(2,1)}, bf16[256,16,256]{0,2,1:T(8,128)(2,1)}, bf16[256,16,256]{0,2,1:T(8,128)(2,1)}, bf16[256,16,256]{0,2,1:T(8,128)(2,1)}) fusion(bf16[256,16,256]{0,2,1:T(8,128)(2,1)S(1)} %copy.257, f32[16,256]{1,0:T(8,128)S(1)} %mul.267, bf16[128,16,256]{0,2,1:T(8,128)(2,1)} %copy.217, bf16[127,16,256]{0,2,1:T(8,128)(2,1)} %copy.259, ...), kind=kLoop, calls=%fused_computation.40 | loop fusion | flops 20971520 | bytes 12648448 | tf_op jit(solution)/shard_map/convert_element_type | solution.py:41
  192.8 3.0 collective-permute-start.3
  197.6 4.5 %collective-permute-start.4 = (f32[4,64]{1,0:T(4,128)S(1)}, f32[4,64]{1,0:T(4,128)S(1)}, u32[]{:S(2)}, u32[]{:S(2)}) collective-permute-start(f32[4,64]{1,0:T(4,128)S(1)} %get-tuple-element.146), channel_id=1, source_target_pairs={{0,64},{16,80},{32,96},{48,112},{64,128},{80,144},{96,160},{112,17... | collective-permute-start | bytes 3080 | tf_op jit(solution)/shard_map/ppermute | solution.py:23
  205.7 7.3 %collective-permute-start.5 = (f32[4,64]{1,0:T(4,128)S(1)}, f32[4,64]{1,0:T(4,128)S(1)}, u32[]{:S(2)}, u32[]{:S(2)}) collective-permute-start(f32[4,64]{1,0:T(4,128)S(1)} %get-tuple-element.144), channel_id=1, source_target_pairs={{0,128},{16,144},{32,160},{48,176},{64,192},{80,208},{96,224},{112... | collective-permute-start | bytes 3080 | tf_op jit(solution)/shard_map/ppermute | solution.py:23
  212.9 5.8 %fusion.62 = (bf16[1,16,2,128,256]{4,3,0,1,2:T(8,128)(2,1)}, bf16[1,16,2,128,256]{4,3,0,1,2:T(8,128)(2,1)S(1)}, bf16[1,16,2,128,256]{4,3,0,1,2:T(8,128)(2,1)S(1)...) fusion(bf16[5,16,2,128,256]{4,3,0,1,2:T(8,128)(2,1)} %bitcast.163), kind=kLoop, calls=%fused_computation.146 | loop fusion | bytes 20971520 | tf_op jit(solution)/shard_map/slice | solution.py:172
  228.3 18.7 %while.13 = (s32[]{:T(128)}, f32[4,64,64]{2,1,0:T(8,128)S(1)}, f32[2,64,4,64]{1,0,3,2:T(2,128)}, f32[2,64,4,64]{1,0,3,2:T(2,128)S(1)}, f32[2,64,4,64]{3,2,1,0:T(...) while((s32[]{:T(128)}, f32[4,64,64]{2,1,0:T(8,128)S(1)}, ...), condition=%wide.region_3.4_spmd.clone, body=%wide.region_0.3_spmd.clone.sunk | while | flops 51646208 | bytes 2444424 | solution.py:101
  233.3 4.3 %dynamic_update_slice.6 = f32[2,64,4,64]{1,0,3,2:T(2,128)} dynamic-update-slice(f32[2,64,4,64]{1,0,3,2:T(2,128)} %get-tuple-element.255, f32[1,64,4,64]{1,0,3,2:T(1,128)S(1)} %copy.313, s32[]{:T(128)S(6)} %copy.337, s32[]{:T(128)} %constant.28.clone.1..sunk, s32[]{:T(128)} %constant.28.clone.1..sunk, s32[]{:T(128)} %constant.28.clone.1..sunk) | dynamic-update-slice | bytes 131076 | tf_op jit(solution)/shard_map/while/body/jit(dynamic_update_index_in_dim)/dynamic_update_slice | solution.py:101
  242.7 4.3 %dynamic_update_slice.6 = f32[2,64,4,64]{1,0,3,2:T(2,128)} dynamic-update-slice(f32[2,64,4,64]{1,0,3,2:T(2,128)} %get-tuple-element.255, f32[1,64,4,64]{1,0,3,2:T(1,128)S(1)} %copy.313, s32[]{:T(128)S(6)} %copy.337, s32[]{:T(128)} %constant.28.clone.1..sunk, s32[]{:T(128)} %constant.28.clone.1..sunk, s32[]{:T(128)} %constant.28.clone.1..sunk) | dynamic-update-slice | bytes 131076 | tf_op jit(solution)/shard_map/while/body/jit(dynamic_update_index_in_dim)/dynamic_update_slice | solution.py:101
  253.9 2.7 exponential_multiply_fusion
  256.8 6.2 %collective-permute-start.8 = (f32[4,64,64]{2,1,0:T(8,128)S(1)}, f32[4,64,64]{2,1,0:T(8,128)}, u32[]{:S(2)}, u32[]{:S(2)}) collective-permute-start(f32[4,64,64]{2,1,0:T(8,128)S(1)} %add_select_fusion.4), channel_id=1, source_target_pairs={{0,32},{16,48},{32,64},{48,80},{64,96},{80,112},{96,128},{112,144}... | collective-permute-start | bytes 196616 | tf_op jit(solution)/shard_map/ppermute | solution.py:23
  267.4 3.3 collective-permute-start.9
  271.3 3.1 collective-permute-done.9
  274.5 12.8 %collective-permute-start.10 = (f32[4,64,64]{2,1,0:T(8,128)S(1)}, f32[4,64,64]{2,1,0:T(8,128)}, u32[]{:S(2)}, u32[]{:S(2)}) collective-permute-start(f32[4,64,64]{2,1,0:T(8,128)S(1)} %add_select_fusion.2), channel_id=1, source_target_pairs={{0,128},{16,144},{32,160},{48,176},{64,192},{80,208},{96,224},{112... | collective-permute-start | bytes 196616 | tf_op jit(solution)/shard_map/ppermute | solution.py:23
  290.2 14.0 %collective-permute-start.11 = (f32[4,64,64]{2,1,0:T(8,128)S(1)}, f32[4,64,64]{2,1,0:T(8,128)}, u32[]{:S(2)}, u32[]{:S(2)}) collective-permute-start(f32[4,64,64]{2,1,0:T(8,128)S(1)} %add_select_fusion.1), channel_id=1, source_target_pairs={{0,256},{16,272},{32,288},{48,304},{64,320},{80,336},{96,352},{112... | collective-permute-start | bytes 196616 | tf_op jit(solution)/shard_map/ppermute | solution.py:23
  306.1 3.1 copy.245
  314.3 6.6 %fusion.43 = f32[256,4096]{1,0:T(8,128)} fusion(bf16[4096,256]{1,0:T(8,128)(2,1)} %bitcast.170, f32[256,256]{1,0:T(8,128)S(1)} %copy.244, f32[256,256]{1,0:T(8,128)S(1)} %copy.243, f32[128,256]{1,0:T(8,128)S(1)} %concatenate.41, f32[128,256]{1,0:T(8,128)S(1)} %copy.241, f32[256]{0:T(256)S(1)} %copy-done.32, f32[256]{0:T(256)S(1)} %copy-done.33, ...), kind=kOutput, calls=%fused_computation.87 | convolution fusion | flops 1074528256 | bytes 11274496 | tf_op jit(solution)/shard_map/dot_general | solution.py:248
  325.3 84.3 %reduce-scatter.2.cloned.1.call-done = f32[16,4096]{1,0:T(8,128)} async-done(((f32[256,4096]{1,0:T(8,128)}), f32[16,4096]{1,0:T(8,128)}) %reduce-scatter.2.cloned.1.call-update) | async-done | bytes 262160 | tf_op jit(solution)/shard_map/reduce_scatter | solution.py:247
  (236 shorter events, 95.4 us)
Async XLA Ops:
  7.2 159.2 %copy-start = (bf16[4096,128]{1,0:T(8,128)(2,1)S(1)}, bf16[4096,128]{1,0:T(8,128)(2,1)}, u32[]{:S(2)}) copy-start(bf16[4096,128]{1,0:T(8,128)(2,1)} %param.30) | copy-start | bytes 3145732
  7.2 91.1 %all-gather.5.cloned.1.call-start = ((), (), s32[]{:S(2)}) async-start(), calls=%async_computation.3 | async-start | bytes 5570560 | tf_op jit(solution)/shard_map/all_gather | solution.py:169
  12.4 200.6 %all-gather.7.cloned.1.call-start = ((), (), s32[]{:S(2)}) async-start(), calls=%async_computation.4 | async-start | bytes 15728640 | tf_op jit(solution)/shard_map/all_gather | solution.py:169
  99.1 2.1 collective-permute-start
  104.4 37.8 %all-to-all-start = ((bf16[257,16,256]{2,0,1:T(8,128)(2,1)}), bf16[257,16,256]{2,0,1:T(8,128)(2,1)S(1)}, u32[]{:S(2)}, u32[]{:S(2)}) async-start(bf16[257,16,256]{2,0,1:T(8,128)(2,1)} %copy.211), calls=%async_computation | async-start | bytes 4325376 | tf_op jit(solution)/shard_map/all_to_all | solution.py:14
  111.7 297.9 %reduce-scatter.2.cloned.1.call-start = ((), (), s32[]{:S(2)}) async-start(), calls=%async_computation.2 | async-start | bytes 4456448 | tf_op jit(solution)/shard_map/reduce_scatter | solution.py:247
  169.8 11.3 %collective-permute-start.1 = (f32[4,64]{1,0:T(4,128)S(1)}, f32[4,64]{1,0:T(4,128)S(1)}, u32[]{:S(2)}, u32[]{:S(2)}) collective-permute-start(f32[4,64]{1,0:T(4,128)S(1)} %reduce_sum.48), channel_id=1, source_target_pairs={{0,16},{16,32},{32,48},{48,64},{64,80},{80,96},{96,112},{112,128},... | collective-permute-start | bytes 3080 | tf_op jit(solution)/shard_map/ppermute | solution.py:23
  181.6 10.6 %collective-permute-start.2 = (f32[4,64]{1,0:T(4,128)S(1)}, f32[4,64]{1,0:T(4,128)S(1)}, u32[]{:S(2)}, u32[]{:S(2)}) collective-permute-start(f32[4,64]{1,0:T(4,128)S(1)} %get-tuple-element.150), channel_id=1, source_target_pairs={{0,16},{16,32},{32,48},{48,64},{64,80},{80,96},{96,112},{112,128},... | collective-permute-start | bytes 3080 | tf_op jit(solution)/shard_map/ppermute | solution.py:23
  192.2 26.6 %copy-start.8 = (f32[2,64,4,64]{3,2,1,0:T(4,128)}, f32[2,64,4,64]{3,2,1,0:T(4,128)S(1)}, u32[]{:S(2)}) copy-start(f32[2,64,4,64]{3,2,1,0:T(4,128)S(1)} %copy.231) | copy-start | bytes 393220
  192.8 4.3 %collective-permute-start.3 = (f32[4,64]{1,0:T(4,128)S(1)}, f32[4,64]{1,0:T(4,128)S(1)}, u32[]{:S(2)}, u32[]{:S(2)}) collective-permute-start(f32[4,64]{1,0:T(4,128)S(1)} %get-tuple-element.148), channel_id=1, source_target_pairs={{0,32},{16,48},{32,64},{48,80},{64,96},{80,112},{96,128},{112,144}... | collective-permute-start | bytes 3080 | tf_op jit(solution)/shard_map/ppermute | solution.py:23
  196.0 22.8 %copy-start.16 = (f32[2,64,4,64]{3,2,1,0:T(4,128)}, f32[2,64,4,64]{3,2,1,0:T(4,128)S(1)}, u32[]{:S(2)}) copy-start(f32[2,64,4,64]{3,2,1,0:T(4,128)S(1)} %fusion.40) | copy-start | bytes 393220
  197.6 7.4 %collective-permute-start.4 = (f32[4,64]{1,0:T(4,128)S(1)}, f32[4,64]{1,0:T(4,128)S(1)}, u32[]{:S(2)}, u32[]{:S(2)}) collective-permute-start(f32[4,64]{1,0:T(4,128)S(1)} %get-tuple-element.146), channel_id=1, source_target_pairs={{0,64},{16,80},{32,96},{48,112},{64,128},{80,144},{96,160},{112,17... | collective-permute-start | bytes 3080 | tf_op jit(solution)/shard_map/ppermute | solution.py:23
  205.7 42.8 %collective-permute-start.5 = (f32[4,64]{1,0:T(4,128)S(1)}, f32[4,64]{1,0:T(4,128)S(1)}, u32[]{:S(2)}, u32[]{:S(2)}) collective-permute-start(f32[4,64]{1,0:T(4,128)S(1)} %get-tuple-element.144), channel_id=1, source_target_pairs={{0,128},{16,144},{32,160},{48,176},{64,192},{80,208},{96,224},{112... | collective-permute-start | bytes 3080 | tf_op jit(solution)/shard_map/ppermute | solution.py:23
  247.0 3.8 collective-permute-start.6
  251.7 4.9 %collective-permute-start.7 = (f32[4,64,64]{2,1,0:T(8,128)S(1)}, f32[4,64,64]{2,1,0:T(8,128)S(1)}, u32[]{:S(2)}, u32[]{:S(2)}) collective-permute-start(f32[4,64,64]{2,1,0:T(8,128)S(1)} %broadcast_select_fusion), channel_id=1, source_target_pairs={{0,16},{16,32},{32,48},{48,64},{64,80},{80,96},{96,112},{112,128},... | collective-permute-start | bytes 196616 | tf_op jit(solution)/shard_map/ppermute | solution.py:23
  256.7 31.4 %copy-start.13 = (f32[128,256]{0,1:T(8,128)S(1)}, f32[128,256]{0,1:T(8,128)}, u32[]{:S(2)}) copy-start(f32[128,256]{0,1:T(8,128)} %copy-done.12) | copy-start | bytes 393220
  256.8 9.6 %collective-permute-start.8 = (f32[4,64,64]{2,1,0:T(8,128)S(1)}, f32[4,64,64]{2,1,0:T(8,128)}, u32[]{:S(2)}, u32[]{:S(2)}) collective-permute-start(f32[4,64,64]{2,1,0:T(8,128)S(1)} %add_select_fusion.4), channel_id=1, source_target_pairs={{0,32},{16,48},{32,64},{48,80},{64,96},{80,112},{96,128},{112,144}... | collective-permute-start | bytes 196616 | tf_op jit(solution)/shard_map/ppermute | solution.py:23
  262.9 26.2 %copy-start.27 = (f32[4,64]{1,0:T(4,128)S(1)}, f32[4,64]{1,0:T(4,128)}, u32[]{:S(2)}) copy-start(f32[4,64]{1,0:T(4,128)} %get-tuple-element.143) | copy-start | bytes 3076
  263.5 40.7 %copy-start.7 = (f32[128,4,64]{2,1,0:T(4,128)S(1)}, f32[128,4,64]{2,1,0:T(4,128)}, u32[]{:S(2)}) copy-start(f32[128,4,64]{2,1,0:T(4,128)} %copy.226) | copy-start | bytes 393220
  267.4 7.0 %collective-permute-start.9 = (f32[4,64,64]{2,1,0:T(8,128)S(1)}, f32[4,64,64]{2,1,0:T(8,128)S(1)}, u32[]{:S(2)}, u32[]{:S(2)}) collective-permute-start(f32[4,64,64]{2,1,0:T(8,128)S(1)} %add_select_fusion.3), channel_id=1, source_target_pairs={{0,64},{16,80},{32,96},{48,112},{64,128},{80,144},{96,160},{112,17... | collective-permute-start | bytes 196616 | tf_op jit(solution)/shard_map/ppermute | solution.py:23
  274.5 14.7 %collective-permute-start.10 = (f32[4,64,64]{2,1,0:T(8,128)S(1)}, f32[4,64,64]{2,1,0:T(8,128)}, u32[]{:S(2)}, u32[]{:S(2)}) collective-permute-start(f32[4,64,64]{2,1,0:T(8,128)S(1)} %add_select_fusion.2), channel_id=1, source_target_pairs={{0,128},{16,144},{32,160},{48,176},{64,192},{80,208},{96,224},{112... | collective-permute-start | bytes 196616 | tf_op jit(solution)/shard_map/ppermute | solution.py:23
  290.2 21.8 %copy-start.14 = (f32[4,64,64]{2,1,0:T(8,128)}, f32[4,64,64]{2,1,0:T(8,128)S(1)}, u32[]{:S(2)}) copy-start(f32[4,64,64]{2,1,0:T(8,128)S(1)} %add_select_fusion.1) | copy-start | bytes 196612
  290.2 21.8 %collective-permute-start.11 = (f32[4,64,64]{2,1,0:T(8,128)S(1)}, f32[4,64,64]{2,1,0:T(8,128)}, u32[]{:S(2)}, u32[]{:S(2)}) collective-permute-start(f32[4,64,64]{2,1,0:T(8,128)S(1)} %add_select_fusion.1), channel_id=1, source_target_pairs={{0,256},{16,272},{32,288},{48,304},{64,320},{80,336},{96,352},{112... | collective-permute-start | bytes 196616 | tf_op jit(solution)/shard_map/ppermute | solution.py:23
  320.9 90.3 %copy-start.1 = (bf16[4096,128]{1,0:T(8,128)(2,1)S(1)}, bf16[4096,128]{1,0:T(8,128)(2,1)}, u32[]{:S(2)}) copy-start(bf16[4096,128]{1,0:T(8,128)(2,1)} %param.30) | copy-start | bytes 3145732
  (28 other events, 168.3 us)
Sparse Core Ops, SparseCore 0:
  12.5 85.6 all-gather.4
  100.3 29.2 all-gather.6
  321.1 88.4 reduce-scatter.1
